TPU v7x, 128 devices: a whole 4x4x4 slice. The times are simulated.
128 devices in a mesh: row: 8 (over y, core), col: 16 (over x, z).
Axes of the slice: x: 4, y: 4, z: 4, core: 2. Of those that a mesh axis runs over, the one named last changes fastest.
Arguments:
- tile_data: float32 [8, 16, 288, 128, 128], P('row', 'col'), as said below
- tile_rows: int32 [8, 16, 288], P('row', 'col'), may hold values from 0 to 2047, as said below
- tile_cols: int32 [8, 16, 288], P('row', 'col'), may hold values from 0 to 1023, as said below
- tile_counts: int32 [8, 16], P('row', 'col'), may hold values from 128 to 288, as said below
Outputs:
- row_scale: float32 [2097152], P('row')
- column_scale: float32 [2097152], P('col')
Inputs may be any that keep to these rules, and one draw needn't show every extreme that they name: `tile_rows`: within one device the blocks of the slots are all different. Slot k < 128 of device (p, q) holds row block q * 128 + k and column block p * 128 + k, so every row and column of A meets a used slot. `tile_cols`: column blocks of the slots, as above. `tile_counts`: some device uses all 288 slots in every draw. `tile_data`: entries are nonzero reals whose tiles have row and column scales of differing sizes.
All inputs are finite; a program needn't handle non-finite values.
Results may differ from a plain program's by a relative error of at most 0.0001.
Values sent between devices are 32-bit elements; how exact they have to be, the bound alone decides.
A program may use at most 64 MiB of HBM per device.

v0:
```python
import jax
import jax.numpy as jnp
from jax import lax
from jax.sharding import PartitionSpec as P

DIAG = 128
SWEEPS = 4
epsilon = 1e-06


def local_terms(magnitude, row_blocks, column_blocks, row_scale, column_scale, want_peak):
    scaled = magnitude * row_scale[row_blocks][:, :, None] * column_scale[column_blocks][:, None, :]
    if want_peak:
        return (scaled.max(axis=2), scaled.max(axis=1))
    return (scaled.sum(axis=2), scaled.sum(axis=1))


def peak_rows(terms, row_blocks, length):
    empty = jnp.zeros((length, terms.shape[1]), jnp.float32)
    return lax.pmax(empty.at[row_blocks].max(terms), "col")


def peak_columns(terms, column_blocks, length):
    empty = jnp.zeros((length, terms.shape[1]), jnp.float32)
    return lax.pmax(empty.at[column_blocks].max(terms), "row")


def total_rows(terms, row_blocks, length):
    empty = jnp.zeros((length, terms.shape[1]), jnp.float32)
    return lax.psum(empty.at[row_blocks].add(terms), "col")


def total_columns(terms, column_blocks, length):
    empty = jnp.zeros((length, terms.shape[1]), jnp.float32)
    return lax.psum(empty.at[column_blocks].add(terms), "row")


def on_device(tile_data, tile_rows, tile_cols, tile_counts):
    blocks = tile_data[0, 0]
    row_blocks = tile_rows[0, 0]
    column_blocks = tile_cols[0, 0]
    used_count = tile_counts[0, 0]
    slots = blocks.shape[0]
    side = blocks.shape[1]
    row_length = DIAG * lax.axis_size("col")
    column_length = DIAG * lax.axis_size("row")
    in_use = jnp.arange(slots, dtype=jnp.int32) < used_count
    magnitude = jnp.where(in_use[:, None, None], jnp.abs(blocks), jnp.float32(0.0))
    row_scale = jnp.ones((row_length, side), jnp.float32)
    column_scale = jnp.ones((column_length, side), jnp.float32)
    for sweep in range(SWEEPS):
        row_terms, column_terms = local_terms(
            magnitude, row_blocks, column_blocks, row_scale, column_scale, True
        )
        peak_row = peak_rows(row_terms, row_blocks, row_length)
        peak_col = peak_columns(column_terms, column_blocks, column_length)
        row_scale = row_scale * lax.rsqrt(peak_row + epsilon)
        column_scale = column_scale * lax.rsqrt(peak_col + epsilon)
    row_terms, column_terms = local_terms(
        magnitude, row_blocks, column_blocks, row_scale, column_scale, False
    )
    total_row = total_rows(row_terms, row_blocks, row_length)
    total_col = total_columns(column_terms, column_blocks, column_length)
    row_scale = row_scale * lax.rsqrt(total_row + epsilon)
    column_scale = column_scale * lax.rsqrt(total_col + epsilon)
    return (row_scale.reshape(-1), column_scale.reshape(-1))


def solution(mesh):
    placed = (
        P("row", "col", None, None, None),
        P("row", "col", None),
        P("row", "col", None),
        P("row", "col"),
    )
    return jax.shard_map(
        on_device, mesh=mesh, in_specs=placed, out_specs=(P("row"), P("col")), check_vma=False
    )
```

profile of v0, /device:TPU:0, one launch (start us, length us, event | category | flops | bytes accessed | tf_op | source)
XLA Modules:
  0.0 876.4 jit_solution(11298934996179545294)
XLA Ops:
  7.2 0.0 all-reduce.13.cloned.1.call-start
  7.9 0.7 fusion.30
  8.6 0.7 fusion.31
  9.3 1.1 gather_fusion.1
  10.4 0.1 broadcast_in_dim.18
  10.5 1.1 gather_fusion
  11.6 15.0 %fusion.1 = (f32[288,128]{1,0:T(8,128)S(1)}, f32[288,128]{1,0:T(8,128)S(1)}) fusion(f32[288,128]{1,0:T(8,128)S(1)} %gather_fusion.1, f32[288,128]{1,0:T(8,128)S(1)} %gather_fusion, f32[1,1,288,128,128]{4,3,2,1,0:T(8,128)} %param.4, pred[288]{0:T(512)(128)(4,1)S(1)} %iota_compare_fusion), kind=kLoop, calls=%fused_computation.27 | loop fusion | flops 28237824 | bytes 19464480 | tf_op jit(solution)/shard_map/reduce_max | solution.py:14
  26.6 2.3 scatter_custom_fusion.1
  28.9 0.0 all-reduce.13.cloned.1.call-update
  28.9 0.0 all-reduce.11.cloned.1.call-start
  29.0 2.5 scatter_custom_fusion
  31.5 0.0 all-reduce.11.cloned.1.call-update
  31.5 0.0 all-reduce.17.cloned.1.call-start
  31.6 61.3 %all-reduce.13.cloned.1.call-done = f32[1024,128]{1,0:T(8,128)} async-done(((f32[1024,128]{1,0:T(8,128)}), f32[1024,128]{1,0:T(8,128)}) %all-reduce.13.cloned.1.call-update) | async-done | bytes 524304 | tf_op jit(solution)/shard_map/pmax | solution.py:25
  92.9 1.2 add_rsqrt_fusion.1
  94.1 1.1 gather_fusion.3
  95.2 88.2 %all-reduce.11.cloned.1.call-done = f32[2048,128]{1,0:T(8,128)} async-done(((f32[2048,128]{1,0:T(8,128)}), f32[2048,128]{1,0:T(8,128)}) %all-reduce.11.cloned.1.call-update) | async-done | bytes 1048592 | tf_op jit(solution)/shard_map/pmax | solution.py:20
  183.4 1.5 add_rsqrt_fusion
  184.9 1.1 gather_fusion.2
  185.9 15.0 %fusion.2 = (f32[288,128]{1,0:T(8,128)S(1)}, f32[288,128]{1,0:T(8,128)S(1)}) fusion(f32[288,128]{1,0:T(8,128)S(1)} %gather_fusion.3, f32[288,128]{1,0:T(8,128)S(1)} %gather_fusion.2, f32[1,1,288,128,128]{4,3,2,1,0:T(8,128)} %param.4, pred[288]{0:T(512)(128)(4,1)S(1)} %iota_compare_fusion), kind=kLoop, calls=%fused_computation.28 | loop fusion | flops 28237824 | bytes 19464480 | tf_op jit(solution)/shard_map/reduce_max | solution.py:14
  201.0 2.3 scatter_custom_fusion.3
  203.3 0.0 all-reduce.17.cloned.1.call-update
  203.3 0.0 all-reduce.15.cloned.1.call-start
  203.4 2.5 scatter_custom_fusion.2
  205.9 0.0 all-reduce.15.cloned.1.call-update
  205.9 0.0 all-reduce.21.cloned.1.call-start
  205.9 58.1 %all-reduce.17.cloned.1.call-done = f32[1024,128]{1,0:T(8,128)} async-done(((f32[1024,128]{1,0:T(8,128)}), f32[1024,128]{1,0:T(8,128)}) %all-reduce.17.cloned.1.call-update) | async-done | bytes 524304 | tf_op jit(solution)/shard_map/pmax | solution.py:25
  264.0 1.2 rsqrt_multiply_fusion.5
  265.2 1.1 gather_fusion.5
  266.3 88.1 %all-reduce.15.cloned.1.call-done = f32[2048,128]{1,0:T(8,128)} async-done(((f32[2048,128]{1,0:T(8,128)}), f32[2048,128]{1,0:T(8,128)}) %all-reduce.15.cloned.1.call-update) | async-done | bytes 1048592 | tf_op jit(solution)/shard_map/pmax | solution.py:20
  354.4 1.5 rsqrt_multiply_fusion.2
  355.9 1.1 gather_fusion.4
  357.0 15.0 %fusion.4 = (f32[288,128]{1,0:T(8,128)S(1)}, f32[288,128]{1,0:T(8,128)S(1)}) fusion(f32[288,128]{1,0:T(8,128)S(1)} %gather_fusion.5, f32[288,128]{1,0:T(8,128)S(1)} %gather_fusion.4, f32[1,1,288,128,128]{4,3,2,1,0:T(8,128)} %param.4, pred[288]{0:T(512)(128)(4,1)S(1)} %iota_compare_fusion), kind=kLoop, calls=%fused_computation.30 | loop fusion | flops 28237824 | bytes 19464480 | tf_op jit(solution)/shard_map/reduce_max | solution.py:14
  372.0 2.3 scatter_custom_fusion.5
  374.3 0.0 all-reduce.21.cloned.1.call-update
  374.3 0.2 all-reduce.19.cloned.1.call-start
  374.6 2.5 scatter_custom_fusion.4
  377.1 0.0 all-reduce.19.cloned.1.call-update
  377.1 0.0 all-reduce.25.cloned.1.call-start
  377.2 57.9 %all-reduce.21.cloned.1.call-done = f32[1024,128]{1,0:T(8,128)} async-done(((f32[1024,128]{1,0:T(8,128)}), f32[1024,128]{1,0:T(8,128)}) %all-reduce.21.cloned.1.call-update) | async-done | bytes 524304 | tf_op jit(solution)/shard_map/pmax | solution.py:25
  435.1 1.1 rsqrt_multiply_fusion.4
  436.2 1.1 gather_fusion.7
  437.2 88.2 %all-reduce.19.cloned.1.call-done = f32[2048,128]{1,0:T(8,128)} async-done(((f32[2048,128]{1,0:T(8,128)}), f32[2048,128]{1,0:T(8,128)}) %all-reduce.19.cloned.1.call-update) | async-done | bytes 1048592 | tf_op jit(solution)/shard_map/pmax | solution.py:20
  525.4 1.4 rsqrt_multiply_fusion.1
  526.8 1.1 gather_fusion.6
  527.8 15.0 %fusion.6 = (f32[288,128]{1,0:T(8,128)S(1)}, f32[288,128]{1,0:T(8,128)S(1)}) fusion(f32[288,128]{1,0:T(8,128)S(1)} %gather_fusion.7, f32[288,128]{1,0:T(8,128)S(1)} %gather_fusion.6, f32[1,1,288,128,128]{4,3,2,1,0:T(8,128)} %param.4, pred[288]{0:T(512)(128)(4,1)S(1)} %iota_compare_fusion), kind=kLoop, calls=%fused_computation.32 | loop fusion | flops 28237824 | bytes 19464480 | tf_op jit(solution)/shard_map/reduce_max | solution.py:14
  542.9 2.3 scatter_custom_fusion.7
  545.2 0.0 all-reduce.23.cloned.1.call-start
  545.3 2.5 scatter_custom_fusion.6
  547.8 0.0 all-reduce.29.cloned.1.call-start
  547.9 58.1 %all-reduce.25.cloned.1.call-done = f32[1024,128]{1,0:T(8,128)} async-done(((f32[1024,128]{1,0:T(8,128)}), f32[1024,128]{1,0:T(8,128)}) %all-reduce.25.cloned.1.call-update) | async-done | bytes 524304 | tf_op jit(solution)/shard_map/pmax | solution.py:25
  605.9 1.1 rsqrt_multiply_fusion.3
  607.1 1.1 gather_fusion.9
  608.1 88.3 %all-reduce.23.cloned.1.call-done = f32[2048,128]{1,0:T(8,128)} async-done(((f32[2048,128]{1,0:T(8,128)}), f32[2048,128]{1,0:T(8,128)}) %all-reduce.23.cloned.1.call-update) | async-done | bytes 1048592 | tf_op jit(solution)/shard_map/pmax | solution.py:20
  696.4 1.4 rsqrt_multiply_fusion
  697.8 1.1 gather_fusion.8
  698.9 15.1 %fusion.8 = (f32[288,128]{1,0:T(8,128)S(1)}, f32[288,128]{1,0:T(8,128)S(1)}) fusion(f32[288,128]{1,0:T(8,128)S(1)} %gather_fusion.9, f32[288,128]{1,0:T(8,128)S(1)} %gather_fusion.8, f32[1,1,288,128,128]{4,3,2,1,0:T(8,128)} %param.4, pred[288]{0:T(512)(128)(4,1)S(1)} %iota_compare_fusion), kind=kLoop, calls=%fused_computation.34 | loop fusion | flops 28237824 | bytes 19464480 | tf_op jit(solution)/shard_map/reduce_sum | solution.py:15
  714.0 2.3 scatter_custom_fusion.9
  716.3 0.0 all-reduce.27.cloned.1.call-start
  716.4 2.5 scatter_custom_fusion.8
  718.9 58.0 %all-reduce.29.cloned.1.call-done = f32[1024,128]{1,0:T(8,128)} async-done(((f32[1024,128]{1,0:T(8,128)}), f32[1024,128]{1,0:T(8,128)}) %all-reduce.29.cloned.1.call-update) | async-done | bytes 524304 | tf_op jit(solution)/shard_map/psum | solution.py:35
  776.9 1.9 multiply_bitcast_fusion.1
  778.8 88.4 %all-reduce.27.cloned.1.call-done = f32[2048,128]{1,0:T(8,128)} async-done(((f32[2048,128]{1,0:T(8,128)}), f32[2048,128]{1,0:T(8,128)}) %all-reduce.27.cloned.1.call-update) | async-done | bytes 1048592 | tf_op jit(solution)/shard_map/psum | solution.py:30
  867.2 2.3 multiply_bitcast_fusion
  (12 shorter events, 0.1 us)
Async XLA Ops:
  7.2 85.7 %all-reduce.13.cloned.1.call-start = ((), (), s32[]{:S(2)}) async-start(), calls=%async_computation.1 | async-start | bytes 1048576 | tf_op jit(solution)/shard_map/pmax | solution.py:25
  28.9 154.5 %all-reduce.11.cloned.1.call-start = ((), (), s32[]{:S(2)}) async-start(), calls=%async_computation | async-start | bytes 2097152 | tf_op jit(solution)/shard_map/pmax | solution.py:20
  31.5 232.5 %all-reduce.17.cloned.1.call-start = ((), (), s32[]{:S(2)}) async-start(), calls=%async_computation.3 | async-start | bytes 1048576 | tf_op jit(solution)/shard_map/pmax | solution.py:25
  92.9 171.1 %copy-start.1 = (f32[1024,128]{1,0:T(8,128)S(1)}, f32[1024,128]{1,0:T(8,128)}, u32[]{:S(2)}) copy-start(f32[1024,128]{1,0:T(8,128)} %all-reduce.13.cloned.1.call-done) | copy-start | bytes 1572868
  183.4 171.0 %copy-start = (f32[2048,128]{1,0:T(8,128)S(1)}, f32[2048,128]{1,0:T(8,128)}, u32[]{:S(2)}) copy-start(f32[2048,128]{1,0:T(8,128)} %all-reduce.11.cloned.1.call-done) | copy-start | bytes 3145732
  203.3 151.1 %all-reduce.15.cloned.1.call-start = ((), (), s32[]{:S(2)}) async-start(), calls=%async_computation.2 | async-start | bytes 2097152 | tf_op jit(solution)/shard_map/pmax | solution.py:20
  205.9 229.2 %all-reduce.21.cloned.1.call-start = ((), (), s32[]{:S(2)}) async-start(), calls=%async_computation.5 | async-start | bytes 1048576 | tf_op jit(solution)/shard_map/pmax | solution.py:25
  374.3 151.1 %all-reduce.19.cloned.1.call-start = ((), (), s32[]{:S(2)}) async-start(), calls=%async_computation.4 | async-start | bytes 2097152 | tf_op jit(solution)/shard_map/pmax | solution.py:20
  377.1 228.8 %all-reduce.25.cloned.1.call-start = ((), (), s32[]{:S(2)}) async-start(), calls=%async_computation.7 | async-start | bytes 1048576 | tf_op jit(solution)/shard_map/pmax | solution.py:25
  545.2 151.2 %all-reduce.23.cloned.1.call-start = ((), (), s32[]{:S(2)}) async-start(), calls=%async_computation.6 | async-start | bytes 2097152 | tf_op jit(solution)/shard_map/pmax | solution.py:20
  547.8 229.1 %all-reduce.29.cloned.1.call-start = ((), (), s32[]{:S(2)}) async-start(), calls=%async_computation.9 | async-start | bytes 1048576 | tf_op jit(solution)/shard_map/psum | solution.py:35
  716.3 150.9 %all-reduce.27.cloned.1.call-start = ((), (), s32[]{:S(2)}) async-start(), calls=%async_computation.8 | async-start | bytes 2097152 | tf_op jit(solution)/shard_map/psum | solution.py:30
Sparse Core Ops, SparseCore 0:
  29.1 63.8 all-reduce.12
  96.7 86.6 all-reduce.10
  203.4 60.5 all-reduce.16
  267.7 86.6 all-reduce.14
  374.5 60.5 all-reduce.20
  438.7 86.6 all-reduce.18
  545.3 60.5 all-reduce.24
  609.8 86.6 all-reduce.22
  716.4 60.3 all-reduce.28
  780.6 86.5 all-reduce.26
where the time goes:
time: 877 us; the launch traced here: 876 us
  waiting for transfers between devices  735 us (84%)
  other arithmetic  115 us (13%)
  between operations  15 us (2%)
  local copies, waits for them, and re-layouts  10.7 us (1%)
    pmax x4, waiting for transfers between devices, peak_rows(): return lax.pmax(empty.at[row_blocks].max(terms), 'col')  353 us
    pmax x4, waiting for transfers between devices, peak_columns(): return lax.pmax(empty.at[column_blocks].max(terms), 'row')  235 us
    psum x1, waiting for transfers between devices, total_rows(): return lax.psum(empty.at[row_blocks].add(terms), 'col')  88.4 us
    reduce_max x4, other arithmetic, local_terms(): return (scaled.max(axis=2), scaled.max(axis=1))  60.2 us
    psum x1, waiting for transfers between devices, total_columns(): return lax.psum(empty.at[column_blocks].add(terms), 'row')  58 us
  transfers between devices with their start and end apart: 10, of which 10 were waited for; matrix products, arithmetic and copies ran while one was open for 3% of the time, Pallas kernels for 0%

commit v1 on v0

--- a/solution.py
+++ b/solution.py
@@ -27,7 +27,8 @@
 
 def total_rows(terms, row_blocks, length):
     empty = jnp.zeros((length, terms.shape[1]), jnp.float32)
-    return lax.psum(empty.at[row_blocks].add(terms), "col")
+    point_screen = lambda t0: jnp.sum(jax.lax.all_gather(t0, "col"), axis=0)
+    return point_screen(empty.at[row_blocks].add(terms))
 
 
 def total_columns(terms, column_blocks, length):

time: 877 us -> 906 us (1.033)
  waiting for transfers between devices: 735 us -> 757 us
    all_gather x0 -> x1, waiting for transfers between devices: none -> 111 us  [total_rows(): point_screen = lambda t0: jnp.sum(jax.lax.all_gather(t0, 'col'), axis=0)]
    psum x1 -> x0, waiting for transfers between devices: 88.4 us -> none  [total_rows(): return lax.psum(empty.at[row_blocks].add(terms), 'col')]
where the time goes in v1:
time: 906 us; the launch traced here: 905 us
  waiting for transfers between devices  757 us (84%)
  other arithmetic  121 us (13%)
  between operations  15 us (2%)
  local copies, waits for them, and re-layouts  10.7 us (1%)
    pmax x4, waiting for transfers between devices, peak_rows(): return lax.pmax(empty.at[row_blocks].max(terms), 'col')  353 us
    pmax x4, waiting for transfers between devices, peak_columns(): return lax.pmax(empty.at[column_blocks].max(terms), 'row')  235 us
    all_gather x1, waiting for transfers between devices, total_rows(): point_screen = lambda t0: jnp.sum(jax.lax.all_gather(t0, 'col'), axis=0)  111 us
    reduce_max x4, other arithmetic, local_terms(): return (scaled.max(axis=2), scaled.max(axis=1))  60.2 us
    psum x1, waiting for transfers between devices, total_columns(): return lax.psum(empty.at[column_blocks].add(terms), 'row')  58 us
  transfers between devices with their start and end apart: 10, of which 10 were waited for; matrix products, arithmetic and copies ran while one was open for 3% of the time, Pallas kernels for 0%

profile of v1, /device:TPU:0, one launch (start us, length us, event | category | flops | bytes accessed | tf_op | source)
XLA Modules:
  0.0 904.6 jit_solution(18188700338756795221)
XLA Ops:
  7.2 0.0 all-reduce.12.cloned.1.call-start
  7.9 0.7 fusion.30
  8.6 0.7 fusion.31
  9.3 1.1 gather_fusion.1
  10.4 0.1 broadcast_in_dim.18
  10.5 1.1 gather_fusion
  11.6 15.0 %fusion.1 = (f32[288,128]{1,0:T(8,128)S(1)}, f32[288,128]{1,0:T(8,128)S(1)}) fusion(f32[288,128]{1,0:T(8,128)S(1)} %gather_fusion.1, f32[288,128]{1,0:T(8,128)S(1)} %gather_fusion, f32[1,1,288,128,128]{4,3,2,1,0:T(8,128)} %param.4, pred[288]{0:T(512)(128)(4,1)S(1)} %iota_compare_fusion), kind=kLoop, calls=%fused_computation.27 | loop fusion | flops 28237824 | bytes 19464480 | tf_op jit(solution)/shard_map/reduce_max | solution.py:14
  26.6 2.3 scatter_custom_fusion.1
  28.9 0.0 all-reduce.12.cloned.1.call-update
  28.9 0.0 all-reduce.10.cloned.1.call-start
  29.0 2.5 scatter_custom_fusion
  31.5 0.0 all-reduce.10.cloned.1.call-update
  31.5 0.0 all-reduce.16.cloned.1.call-start
  31.6 61.3 %all-reduce.12.cloned.1.call-done = f32[1024,128]{1,0:T(8,128)} async-done(((f32[1024,128]{1,0:T(8,128)}), f32[1024,128]{1,0:T(8,128)}) %all-reduce.12.cloned.1.call-update) | async-done | bytes 524304 | tf_op jit(solution)/shard_map/pmax | solution.py:25
  92.9 1.2 add_rsqrt_fusion.1
  94.1 1.1 gather_fusion.3
  95.2 88.2 %all-reduce.10.cloned.1.call-done = f32[2048,128]{1,0:T(8,128)} async-done(((f32[2048,128]{1,0:T(8,128)}), f32[2048,128]{1,0:T(8,128)}) %all-reduce.10.cloned.1.call-update) | async-done | bytes 1048592 | tf_op jit(solution)/shard_map/pmax | solution.py:20
  183.4 1.5 add_rsqrt_fusion
  184.9 1.1 gather_fusion.2
  185.9 15.0 %fusion.2 = (f32[288,128]{1,0:T(8,128)S(1)}, f32[288,128]{1,0:T(8,128)S(1)}) fusion(f32[288,128]{1,0:T(8,128)S(1)} %gather_fusion.3, f32[288,128]{1,0:T(8,128)S(1)} %gather_fusion.2, f32[1,1,288,128,128]{4,3,2,1,0:T(8,128)} %param.4, pred[288]{0:T(512)(128)(4,1)S(1)} %iota_compare_fusion), kind=kLoop, calls=%fused_computation.28 | loop fusion | flops 28237824 | bytes 19464480 | tf_op jit(solution)/shard_map/reduce_max | solution.py:14
  201.0 2.3 scatter_custom_fusion.3
  203.3 0.0 all-reduce.16.cloned.1.call-update
  203.3 0.0 all-reduce.14.cloned.1.call-start
  203.4 2.5 scatter_custom_fusion.2
  205.9 0.0 all-reduce.14.cloned.1.call-update
  205.9 0.0 all-reduce.20.cloned.1.call-start
  205.9 58.1 %all-reduce.16.cloned.1.call-done = f32[1024,128]{1,0:T(8,128)} async-done(((f32[1024,128]{1,0:T(8,128)}), f32[1024,128]{1,0:T(8,128)}) %all-reduce.16.cloned.1.call-update) | async-done | bytes 524304 | tf_op jit(solution)/shard_map/pmax | solution.py:25
  264.0 1.2 rsqrt_multiply_fusion.5
  265.2 1.1 gather_fusion.5
  266.3 88.1 %all-reduce.14.cloned.1.call-done = f32[2048,128]{1,0:T(8,128)} async-done(((f32[2048,128]{1,0:T(8,128)}), f32[2048,128]{1,0:T(8,128)}) %all-reduce.14.cloned.1.call-update) | async-done | bytes 1048592 | tf_op jit(solution)/shard_map/pmax | solution.py:20
  354.4 1.5 rsqrt_multiply_fusion.2
  355.9 1.1 gather_fusion.4
  357.0 15.0 %fusion.4 = (f32[288,128]{1,0:T(8,128)S(1)}, f32[288,128]{1,0:T(8,128)S(1)}) fusion(f32[288,128]{1,0:T(8,128)S(1)} %gather_fusion.5, f32[288,128]{1,0:T(8,128)S(1)} %gather_fusion.4, f32[1,1,288,128,128]{4,3,2,1,0:T(8,128)} %param.4, pred[288]{0:T(512)(128)(4,1)S(1)} %iota_compare_fusion), kind=kLoop, calls=%fused_computation.30 | loop fusion | flops 28237824 | bytes 19464480 | tf_op jit(solution)/shard_map/reduce_max | solution.py:14
  372.0 2.3 scatter_custom_fusion.5
  374.3 0.0 all-reduce.20.cloned.1.call-update
  374.3 0.2 all-reduce.18.cloned.1.call-start
  374.6 2.5 scatter_custom_fusion.4
  377.1 0.0 all-reduce.24.cloned.1.call-start
  377.2 57.9 %all-reduce.20.cloned.1.call-done = f32[1024,128]{1,0:T(8,128)} async-done(((f32[1024,128]{1,0:T(8,128)}), f32[1024,128]{1,0:T(8,128)}) %all-reduce.20.cloned.1.call-update) | async-done | bytes 524304 | tf_op jit(solution)/shard_map/pmax | solution.py:25
  435.1 1.1 rsqrt_multiply_fusion.4
  436.2 1.1 gather_fusion.7
  437.2 88.2 %all-reduce.18.cloned.1.call-done = f32[2048,128]{1,0:T(8,128)} async-done(((f32[2048,128]{1,0:T(8,128)}), f32[2048,128]{1,0:T(8,128)}) %all-reduce.18.cloned.1.call-update) | async-done | bytes 1048592 | tf_op jit(solution)/shard_map/pmax | solution.py:20
  525.4 1.4 rsqrt_multiply_fusion.1
  526.8 1.1 gather_fusion.6
  527.8 15.0 %fusion.6 = (f32[288,128]{1,0:T(8,128)S(1)}, f32[288,128]{1,0:T(8,128)S(1)}) fusion(f32[288,128]{1,0:T(8,128)S(1)} %gather_fusion.7, f32[288,128]{1,0:T(8,128)S(1)} %gather_fusion.6, f32[1,1,288,128,128]{4,3,2,1,0:T(8,128)} %param.4, pred[288]{0:T(512)(128)(4,1)S(1)} %iota_compare_fusion), kind=kLoop, calls=%fused_computation.32 | loop fusion | flops 28237824 | bytes 19464480 | tf_op jit(solution)/shard_map/reduce_max | solution.py:14
  542.9 2.3 scatter_custom_fusion.7
  545.2 0.0 all-reduce.22.cloned.1.call-start
  545.3 2.5 scatter_custom_fusion.6
  547.8 0.0 all-reduce.26.cloned.1.call-start
  547.9 58.1 %all-reduce.24.cloned.1.call-done = f32[1024,128]{1,0:T(8,128)} async-done(((f32[1024,128]{1,0:T(8,128)}), f32[1024,128]{1,0:T(8,128)}) %all-reduce.24.cloned.1.call-update) | async-done | bytes 524304 | tf_op jit(solution)/shard_map/pmax | solution.py:25
  605.9 1.1 rsqrt_multiply_fusion.3
  607.1 1.1 gather_fusion.9
  608.1 88.3 %all-reduce.22.cloned.1.call-done = f32[2048,128]{1,0:T(8,128)} async-done(((f32[2048,128]{1,0:T(8,128)}), f32[2048,128]{1,0:T(8,128)}) %all-reduce.22.cloned.1.call-update) | async-done | bytes 1048592 | tf_op jit(solution)/shard_map/pmax | solution.py:20
  696.4 1.4 rsqrt_multiply_fusion
  697.8 1.1 gather_fusion.8
  698.9 15.1 %fusion.8 = (f32[288,128]{1,0:T(8,128)S(1)}, f32[288,128]{1,0:T(8,128)S(1)}) fusion(f32[288,128]{1,0:T(8,128)S(1)} %gather_fusion.9, f32[288,128]{1,0:T(8,128)S(1)} %gather_fusion.8, f32[1,1,288,128,128]{4,3,2,1,0:T(8,128)} %param.4, pred[288]{0:T(512)(128)(4,1)S(1)} %iota_compare_fusion), kind=kLoop, calls=%fused_computation.34 | loop fusion | flops 28237824 | bytes 19464480 | tf_op jit(solution)/shard_map/reduce_sum | solution.py:15
  714.0 2.3 scatter_custom_fusion.9
  716.3 0.0 all-gather.3.cloned.1.call-start
  716.4 2.5 scatter_custom_fusion.8
  718.9 58.0 %all-reduce.26.cloned.1.call-done = f32[1024,128]{1,0:T(8,128)} async-done(((f32[1024,128]{1,0:T(8,128)}), f32[1024,128]{1,0:T(8,128)}) %all-reduce.26.cloned.1.call-update) | async-done | bytes 524304 | tf_op jit(solution)/shard_map/psum | solution.py:36
  776.9 1.9 multiply_bitcast_fusion.1
  778.8 111.2 %all-gather.3.cloned.1.call-done = f32[32768,128]{1,0:T(8,128)} async-done(((f32[2048,128]{1,0:T(8,128)}), f32[32768,128]{1,0:T(8,128)}) %all-gather.3.cloned.1.call-update) | async-done | bytes 16777232 | tf_op jit(solution)/shard_map/all_gather | solution.py:30
  890.0 6.6 reduce_sum.28
  896.6 1.1 multiply_bitcast_fusion
  (13 shorter events, 0.1 us)
Async XLA Ops:
  7.2 85.7 %all-reduce.12.cloned.1.call-start = ((), (), s32[]{:S(2)}) async-start(), calls=%async_computation.1 | async-start | bytes 1048576 | tf_op jit(solution)/shard_map/pmax | solution.py:25
  28.9 154.5 %all-reduce.10.cloned.1.call-start = ((), (), s32[]{:S(2)}) async-start(), calls=%async_computation | async-start | bytes 2097152 | tf_op jit(solution)/shard_map/pmax | solution.py:20
  31.5 232.5 %all-reduce.16.cloned.1.call-start = ((), (), s32[]{:S(2)}) async-start(), calls=%async_computation.3 | async-start | bytes 1048576 | tf_op jit(solution)/shard_map/pmax | solution.py:25
  92.9 171.1 %copy-start.1 = (f32[1024,128]{1,0:T(8,128)S(1)}, f32[1024,128]{1,0:T(8,128)}, u32[]{:S(2)}) copy-start(f32[1024,128]{1,0:T(8,128)} %all-reduce.12.cloned.1.call-done) | copy-start | bytes 1572868
  183.4 171.0 %copy-start = (f32[2048,128]{1,0:T(8,128)S(1)}, f32[2048,128]{1,0:T(8,128)}, u32[]{:S(2)}) copy-start(f32[2048,128]{1,0:T(8,128)} %all-reduce.10.cloned.1.call-done) | copy-start | bytes 3145732
  203.3 151.1 %all-reduce.14.cloned.1.call-start = ((), (), s32[]{:S(2)}) async-start(), calls=%async_computation.2 | async-start | bytes 2097152 | tf_op jit(solution)/shard_map/pmax | solution.py:20
  205.9 229.2 %all-reduce.20.cloned.1.call-start = ((), (), s32[]{:S(2)}) async-start(), calls=%async_computation.5 | async-start | bytes 1048576 | tf_op jit(solution)/shard_map/pmax | solution.py:25
  374.3 151.1 %all-reduce.18.cloned.1.call-start = ((), (), s32[]{:S(2)}) async-start(), calls=%async_computation.4 | async-start | bytes 2097152 | tf_op jit(solution)/shard_map/pmax | solution.py:20
  377.1 228.8 %all-reduce.24.cloned.1.call-start = ((), (), s32[]{:S(2)}) async-start(), calls=%async_computation.7 | async-start | bytes 1048576 | tf_op jit(solution)/shard_map/pmax | solution.py:25
  545.2 151.2 %all-reduce.22.cloned.1.call-start = ((), (), s32[]{:S(2)}) async-start(), calls=%async_computation.6 | async-start | bytes 2097152 | tf_op jit(solution)/shard_map/pmax | solution.py:20
  547.8 229.1 %all-reduce.26.cloned.1.call-start = ((), (), s32[]{:S(2)}) async-start(), calls=%async_computation.8 | async-start | bytes 1048576 | tf_op jit(solution)/shard_map/psum | solution.py:36
  716.3 173.6 %all-gather.3.cloned.1.call-start = ((), (), s32[]{:S(2)}) async-start(), calls=%async_computation.9 | async-start | bytes 17825792 | tf_op jit(solution)/shard_map/all_gather | solution.py:30
Sparse Core Ops, SparseCore 0:
  29.1 63.8 all-reduce.11
  96.7 86.6 all-reduce.9
  203.4 60.5 all-reduce.15
  267.7 86.6 all-reduce.13
  374.5 60.5 all-reduce.19
  438.7 86.6 all-reduce.17
  545.3 60.5 all-reduce.23
  609.8 86.6 all-reduce.21
  716.4 60.3 all-reduce.25
  779.4 110.4 all-gather.2
